TPU v7x, 32 devices: a whole 2x2x4 slice. The times are simulated.
32 devices in a mesh: fsdp: 8 (over z, x), tensor: 2 (over y), dp: 2 (over core).
Axes of the slice: x: 2, y: 2, z: 4, core: 2. Of those that a mesh axis runs over, the one named last changes fastest.
Arguments:
- states: bfloat16 [4096, 4096], P('fsdp', ('tensor', 'dp')), may hold values from -6 to 6
- fresh_rows: bfloat16 [4096, 4096], P('fsdp', ('tensor', 'dp')), may hold values from -6 to 6
- norm_gain: bfloat16 [4096], P(('tensor', 'dp')), may hold values from 0.25 to 1.75
- gate_weight: bfloat16 [4096, 8192], P('fsdp', ('tensor', 'dp')), may hold values from -0.09375 to 0.09375
- up_weight: bfloat16 [4096, 8192], P('fsdp', ('tensor', 'dp')), may hold values from -0.09375 to 0.09375
- down_weight: bfloat16 [8192, 4096], P(('tensor', 'dp'), 'fsdp'), may hold values from -0.09375 to 0.09375
- halted: int32 [64, 64], P('fsdp'), may hold values from 0 to 1, as said below
- refill_index: int32 [64, 64], P('fsdp'), may hold values from 0 to 63, each once within a row
Outputs:
- next_states: bfloat16 [4096, 4096], P('fsdp', ('tensor', 'dp'))
Inputs may be any that keep to these rules, and one draw needn't show every extreme that they name: In each aligned block of 512 rows (in row order over all batches) at most 384 rows are running (halted 0), and some block has exactly 384 running rows. Each batch's row of refill_index holds every number of 0 to 63 once.
All inputs are finite; a program needn't handle non-finite values.
Results may differ from a plain program's by a relative error of at most 0.0085.
Values may be sent and summed in bfloat16 or wider, within the bound.
A program may use at most 128 MiB of HBM per device.

v0:
```python
import jax
import jax.numpy as jnp
from jax import lax
from jax.sharding import PartitionSpec as P

norm_eps = 1e-05


def block_update(source, norm_gain, gate_weight, up_weight, down_weight):
    gathered, gain_full = (
        lax.all_gather(source, ("tensor", "dp"), axis=1, tiled=True),
        lax.all_gather(norm_gain, ("tensor", "dp"), axis=0, tiled=True),
    )
    widened = gathered.astype(jnp.float32)
    mean_square = jnp.mean(widened * widened, axis=-1, keepdims=True)
    normed = (widened * lax.rsqrt(mean_square + norm_eps) * gain_full.astype(jnp.float32)).astype(
        jnp.bfloat16
    )
    gate_more = jnp.dot(
        normed,
        lax.all_gather(gate_weight, "fsdp", axis=0, tiled=True),
        preferred_element_type=jnp.float32,
    )
    up_more = jnp.dot(
        normed,
        lax.all_gather(up_weight, "fsdp", axis=0, tiled=True),
        preferred_element_type=jnp.float32,
    )
    hidden = (jax.nn.silu(gate_more) * up_more).astype(jnp.bfloat16)
    partial_value = jnp.dot(
        hidden,
        lax.all_gather(down_weight, "fsdp", axis=1, tiled=True),
        preferred_element_type=jnp.float32,
    )
    return lax.psum_scatter(
        partial_value.astype(jnp.bfloat16), ("tensor", "dp"), scatter_dimension=1, tiled=True
    ).astype(jnp.float32)


def body(states, fresh_rows, norm_gain, gate_weight, up_weight, down_weight, halted, refill_index):
    row_count = states.shape[0]
    running = halted.reshape(row_count) == 0
    capacity = row_count * 3 // 4
    slot_of = jnp.cumsum(running.astype(jnp.int32)) - 1
    slot_ids = lax.iota(jnp.int32, capacity)
    picker = ((slot_of[None, :] == slot_ids[:, None]) & running[None, :]).astype(jnp.bfloat16)
    source = jnp.dot(picker, states, preferred_element_type=jnp.float32).astype(jnp.bfloat16)
    compact = block_update(source, norm_gain, gate_weight, up_weight, down_weight)
    update = jnp.take(compact, jnp.clip(slot_of, 0, capacity - 1), axis=0)
    block_total = refill_index.shape[0]
    batch_len = refill_index.shape[1]
    fresh_blocks = fresh_rows.reshape(block_total, batch_len, fresh_rows.shape[1])
    refilled = jax.vmap(lambda block_rows, pick_index: block_rows[pick_index])(
        fresh_blocks, refill_index
    )
    refilled = refilled.reshape(row_count, fresh_rows.shape[1])
    computed = (states.astype(jnp.float32) + update).astype(jnp.bfloat16)
    return jnp.where(running[:, None], computed, refilled)


def solution(mesh):
    in_specs = (
        P("fsdp", ("tensor", "dp")),
        P("fsdp", ("tensor", "dp")),
        P(("tensor", "dp")),
        P("fsdp", ("tensor", "dp")),
        P("fsdp", ("tensor", "dp")),
        P(("tensor", "dp"), "fsdp"),
        P("fsdp", None),
        P("fsdp", None),
    )
    out_specs = P("fsdp", ("tensor", "dp"))
    return jax.shard_map(body, mesh=mesh, in_specs=in_specs, out_specs=out_specs, check_vma=False)
```

profile of v0, /device:TPU:0, one launch (start us, length us, event | category | flops | bytes accessed | tf_op | source)
XLA Modules:
  0.0 803.4 jit_solution(10444308348933228802)
XLA Ops:
  6.5 0.8 fusion.21
  7.4 0.3 reduce-window.9
  7.8 0.1 slice_reduce_fusion
  7.9 0.1 compare_and_fusion
  8.0 0.1 eq.40
  8.1 2.7 convolution_convert_fusion.1
  10.9 0.7 all-gather.7.cloned.1.call-update
  11.6 0.7 all-gather.11.cloned.1.call-update
  12.4 0.5 all-gather.9.cloned.1.call-update
  12.9 6.2 all_gather.16
  19.1 23.1 %all-gather.5.cloned.1.call-done = bf16[384,4096]{1,0:T(8,128)(2,1)} async-done(((bf16[384,1024]{1,0:T(8,128)(2,1)}), bf16[384,4096]{1,0:T(8,128)(2,1)}) %all-gather.5.cloned.1.call-update) | async-done | bytes 3145744 | tf_op jit(solution)/shard_map/all_gather | solution.py:11
  42.2 2.6 fusion
  44.8 226.8 %all-gather.7.cloned.1.call-done = bf16[4096,2048]{1,0:T(8,128)(2,1)} async-done(((bf16[512,2048]{1,0:T(8,128)(2,1)}), bf16[4096,2048]{1,0:T(8,128)(2,1)}) %all-gather.7.cloned.1.call-update) | async-done | bytes 16777232 | tf_op jit(solution)/shard_map/all_gather | solution.py:21
  271.6 12.3 %fusion.7 = f32[384,2048]{1,0:T(8,128)} fusion(bf16[4096,2048]{1,0:T(8,128)(2,1)} %all-gather.7.cloned.1.call-done, bf16[384,4096]{1,0:T(8,128)(2,1)} %all-gather.5.cloned.1.call-done, f32[4096]{0:T(1024)S(1)} %convert_element_type.40, f32[384]{0:T(512)S(1)} %add_rsqrt_fusion), kind=kOutput, calls=%fused_computation.13 | convolution fusion | flops 6448742400 | bytes 23086592 | tf_op jit(solution)/shard_map/dot_general | solution.py:19
  284.0 215.2 %all-gather.11.cloned.1.call-done = bf16[2048,4096]{1,0:T(8,128)(2,1)} async-done(((bf16[2048,512]{1,0:T(8,128)(2,1)}), bf16[2048,4096]{1,0:T(8,128)(2,1)}) %all-gather.11.cloned.1.call-update) | async-done | bytes 16777232 | tf_op jit(solution)/shard_map/all_gather | solution.py:32
  499.2 227.5 %all-gather.9.cloned.1.call-done = bf16[4096,2048]{1,0:T(8,128)(2,1)} async-done(((bf16[512,2048]{1,0:T(8,128)(2,1)}), bf16[4096,2048]{1,0:T(8,128)(2,1)}) %all-gather.9.cloned.1.call-update) | async-done | bytes 16777232 | tf_op jit(solution)/shard_map/all_gather | solution.py:26
  726.7 26.5 %convolution_convert_fusion = bf16[384,4096]{1,0:T(8,128)(2,1)} fusion(bf16[2048,4096]{1,0:T(8,128)(2,1)} %all-gather.11.cloned.1.call-done, f32[384,2048]{1,0:T(8,128)} %fusion.7, bf16[4096,2048]{1,0:T(8,128)(2,1)} %all-gather.9.cloned.1.call-done, bf16[384,4096]{1,0:T(8,128)(2,1)} %all-gather.5.cloned.1.call-done, f32[4096]{0:T(1024)S(1)} %convert_element_type.40, ...), kind=kOutput, calls=%fused_computation.7 | convolution fusion | flops 12897484800 | bytes 43009536 | tf_op jit(solution)/shard_map/dot_general | solution.py:30
  753.2 0.7 copy-done.1
  753.9 0.1 reshape.116
  754.0 7.9 gather_fusion.1
  762.0 27.3 %reduce-scatter.2.cloned.1.call-done = bf16[384,1024]{1,0:T(8,128)(2,1)} async-done(((bf16[384,4096]{1,0:T(8,128)(2,1)}), bf16[384,1024]{1,0:T(8,128)(2,1)}) %reduce-scatter.2.cloned.1.call-update) | async-done | bytes 786448 | tf_op jit(solution)/shard_map/reduce_scatter | solution.py:35
  789.3 1.3 convert_element_type.44
  790.6 2.7 gather_fusion
  793.3 3.6 fusion.4
  (21 shorter events, 0.5 us)
Async XLA Ops:
  6.5 747.4 %copy-start = (bf16[512,1024]{1,0:T(8,128)(2,1)S(1)}, bf16[512,1024]{1,0:T(8,128)(2,1)}, u32[]{:S(2)}) copy-start(bf16[512,1024]{1,0:T(8,128)(2,1)} %param.9) | copy-start | bytes 3145732
  6.5 35.7 %all-gather.5.cloned.1.call-start = ((), (), s32[]{:S(2)}) async-start(), calls=%async_computation.1 | async-start | bytes 3932160 | tf_op jit(solution)/shard_map/all_gather | solution.py:11
  10.8 2.1 copy-start.2
  10.8 260.8 %all-gather.7.cloned.1.call-start = ((), (), s32[]{:S(2)}) async-start(), calls=%async_computation.2 | async-start | bytes 18874368 | tf_op jit(solution)/shard_map/all_gather | solution.py:21
  11.6 487.6 %all-gather.11.cloned.1.call-start = ((), (), s32[]{:S(2)}) async-start(), calls=%async_computation.4 | async-start | bytes 18874368 | tf_op jit(solution)/shard_map/all_gather | solution.py:32
  12.3 714.4 %all-gather.9.cloned.1.call-start = ((), (), s32[]{:S(2)}) async-start(), calls=%async_computation.3 | async-start | bytes 18874368 | tf_op jit(solution)/shard_map/all_gather | solution.py:26
  12.9 776.4 %reduce-scatter.2.cloned.1.call-start = ((), (), s32[]{:S(2)}) async-start(), calls=%async_computation.5 | async-start | bytes 3932160 | tf_op jit(solution)/shard_map/reduce_scatter | solution.py:35
  753.2 0.7 copy-start.1
Sparse Core Ops, SparseCore 0:
  10.9 31.2 all-gather.4
  44.3 227.2 all-gather.6
  273.7 225.4 all-gather.10
  501.2 225.4 all-gather.8
  753.3 35.9 reduce-scatter.1
where the time goes:
time: 804 us; the launch traced here: 803 us
  waiting for transfers between devices  722 us (90%)
  matrix products  41.5 us (5%)
  between operations  13.2 us (2%)
  local copies, waits for them, and re-layouts  11.7 us (1%)
  other arithmetic  8.79 us (1%)
    all_gather x1, waiting for transfers between devices, block_update(): lax.all_gather(up_weight, 'fsdp', axis=0, tiled=True)  227 us
    all_gather x1, waiting for transfers between devices, block_update(): lax.all_gather(gate_weight, 'fsdp', axis=0, tiled=True)  227 us
    all_gather x1, waiting for transfers between devices, block_update(): lax.all_gather(down_weight, 'fsdp', axis=1, tiled=True)  215 us
    reduce_scatter x1, waiting for transfers between devices, block_update(): lax.psum_scatter(partial_value.astype(jnp.bfloat16), ('tensor', 'dp'), sc...  27.3 us
    dot_general x1, matrix products, block_update(): jnp.dot(hidden, lax.all_gather(down_weight, 'fsdp', axis=1, tiled=True),...  26.5 us
    all_gather x1, waiting for transfers between devices, block_update(): lax.all_gather(source, ('tensor', 'dp'), axis=1, tiled=True)  23.1 us
  transfers between devices with their start and end apart: 5, of which 5 were waited for; matrix products, arithmetic and copies ran while one was open for 3% of the time, Pallas kernels for 0%

commit v1 on v0

--- a/solution.py
+++ b/solution.py
@@ -4,6 +4,24 @@
 from jax.sharding import PartitionSpec as P
 
 norm_eps = 1e-05
+
+
+def ring_gather(shard, axis, dim):
+    ways, here, lap = (lax.axis_size(axis), lax.axis_index(axis), shard.shape[dim])
+    dims = [n * ways if d == dim else n for d, n in enumerate(shard.shape)]
+    full = lax.dynamic_update_slice_in_dim(
+        jnp.zeros(dims, shard.dtype), shard, here * lap, axis=dim
+    )
+    going_up = going_down = shard
+    for far in range(1, ways // 2 + 1):
+        going_up = lax.ppermute(going_up, axis, [(d, (d + 1) % ways) for d in range(ways)])
+        full = lax.dynamic_update_slice_in_dim(full, going_up, (here - far) % ways * lap, axis=dim)
+        if 2 * far < ways:
+            going_down = lax.ppermute(going_down, axis, [(d, (d - 1) % ways) for d in range(ways)])
+            full = lax.dynamic_update_slice_in_dim(
+                full, going_down, (here + far) % ways * lap, axis=dim
+            )
+    return full
 
 
 def block_update(source, norm_gain, gate_weight, up_weight, down_weight):
@@ -17,9 +35,7 @@
         jnp.bfloat16
     )
     gate_more = jnp.dot(
-        normed,
-        lax.all_gather(gate_weight, "fsdp", axis=0, tiled=True),
-        preferred_element_type=jnp.float32,
+        normed, ring_gather(gate_weight, "fsdp", 0), preferred_element_type=jnp.float32
     )
     up_more = jnp.dot(
         normed,

time: 804 us -> 789 us (0.981)
  waiting for transfers between devices: 722 us -> 647 us
  starting transfers between devices: 0.16 us -> 34.8 us
  local copies, waits for them, and re-layouts: 11.7 us -> 38.2 us
    ppermute x0 -> x7, waiting for transfers between devices: none -> 399 us  [the longest x4 399 us: ring_gather(): lax.ppermute(going_up, axis, [(d, (d + 1) % ways) for d in range(ways)])]
    all_gather x1, waiting for transfers between devices: 227 us -> 0.01 us  [block_update(): lax.all_gather(up_weight, 'fsdp', axis=0, tiled=True)]
    all_gather x1 -> x0, waiting for transfers between devices: 227 us -> none  [block_update(): lax.all_gather(gate_weight, 'fsdp', axis=0, tiled=True)]
    ppermute x0 -> x7, starting transfers between devices: none -> 34.7 us  [the longest x3 24.1 us: ring_gather(): lax.ppermute(going_down, axis, [(d, (d - 1) % ways) for d in range(ways)])]
    all_gather x1, waiting for transfers between devices: 23.1 us -> 0.01 us  [block_update(): lax.all_gather(source, ('tensor', 'dp'), axis=1, tiled=True)]
    dynamic_update_slice x0 -> x8, local copies, waits for them, and re-layouts: none -> 20.5 us  [the longest x3 9.54 us: ring_gather(): lax.dynamic_update_slice_in_dim(full, going_down, (here + far) % ways * l...]
  transfers between devices with their start and end apart: 5 -> 11, of which waited for: 5 -> 6; matrix products, arithmetic and copies ran while one was open for 3% -> 6% of each run, Pallas kernels for 0% -> 0%
where the time goes in v1:
time: 789 us
  waiting for transfers between devices  647 us (82%)
  matrix products  41.6 us (5%)
  local copies, waits for them, and re-layouts  38.2 us (5%)
  starting transfers between devices  34.8 us (4%)
  between operations  13.2 us (2%)
  other arithmetic  8.8 us (1%)
    ppermute x4, waiting for transfers between devices, ring_gather(): lax.ppermute(going_up, axis, [(d, (d + 1) % ways) for d in range(ways)])  399 us
    all_gather x1, waiting for transfers between devices, block_update(): lax.all_gather(down_weight, 'fsdp', axis=1, tiled=True)  220 us
    reduce_scatter x1, waiting for transfers between devices, block_update(): lax.psum_scatter(partial_value.astype(jnp.bfloat16), ('tensor', 'dp'), sc...  27.3 us
    dot_general x1, matrix products, block_update(): jnp.dot(hidden, lax.all_gather(down_weight, 'fsdp', axis=1, tiled=True),...  26.3 us
    ppermute x3, starting transfers between devices, ring_gather(): lax.ppermute(going_down, axis, [(d, (d - 1) % ways) for d in range(ways)])  24.1 us
  transfers between devices with their start and end apart: 11, of which 6 were waited for; matrix products, arithmetic and copies ran while one was open for 6% of the time, Pallas kernels for 0%

profile of v1, /device:TPU:0, one launch (start us, length us, event | category | flops | bytes accessed | tf_op | source)
XLA Modules:
  0.0 789.0 jit_solution(4637743029943535541)
XLA Ops:
  8.1 2.8 convolution_convert_fusion.1
  12.5 3.0 collective-permute-start
  15.5 3.1 collective-permute-start.1
  18.6 109.2 %collective-permute-done = bf16[512,2048]{1,0:T(8,128)(2,1)S(1)} collective-permute-done((bf16[512,2048]{1,0:T(8,128)(2,1)S(1)}, bf16[512,2048]{1,0:T(8,128)(2,1)S(1)}, u32[]{:S(2)}, u32[]{:S(2)}) %collective-permute-start) | collective-permute-done | bytes 2097184 | tf_op jit(solution)/shard_map/ppermute | solution.py:17
  130.3 4.3 collective-permute-start.3
  134.7 124.7 %collective-permute-done.2 = bf16[512,2048]{1,0:T(8,128)(2,1)} collective-permute-done((bf16[512,2048]{1,0:T(8,128)(2,1)S(1)}, bf16[512,2048]{1,0:T(8,128)(2,1)}, u32[]{:S(2)}, u32[]{:S(2)}) %collective-permute-start.2) | collective-permute-done | bytes 2097184 | tf_op jit(solution)/shard_map/ppermute | solution.py:17
  259.4 2.6 collective-permute-start.4
  261.9 5.2 all_gather.13
  267.1 16.6 %collective-permute-start.5 = (bf16[512,2048]{1,0:T(8,128)(2,1)}, bf16[512,2048]{1,0:T(8,128)(2,1)}, u32[]{:S(2)}, u32[]{:S(2)}) collective-permute-start(bf16[512,2048]{1,0:T(8,128)(2,1)} %collective-permute-done.3), channel_id=1, source_target_pairs={{0,28},{4,0},{8,4},{12,8},{16,12},{20,16},{24,20},{28,24},{1,29},{... | collective-permute-start | bytes 6291464 | tf_op jit(solution)/shard_map/ppermute | solution.py:20
  283.8 6.0 broadcast_in_dim.32
  291.3 105.8 %collective-permute-done.4 = bf16[512,2048]{1,0:T(8,128)(2,1)} collective-permute-done((bf16[512,2048]{1,0:T(8,128)(2,1)}, bf16[512,2048]{1,0:T(8,128)(2,1)}, u32[]{:S(2)}, u32[]{:S(2)}) %collective-permute-start.4) | collective-permute-done | bytes 2097184 | tf_op jit(solution)/shard_map/ppermute | solution.py:17
  401.1 3.2 constant_dynamic-update-slice_fusion.5
  404.3 3.2 constant_dynamic-update-slice_fusion.4
  407.5 3.1 constant_dynamic-update-slice_fusion.3
  413.2 3.2 constant_dynamic-update-slice_fusion.2
  416.4 3.2 constant_dynamic-update-slice_fusion.1
  419.6 59.4 %collective-permute-done.6 = bf16[512,2048]{1,0:T(8,128)(2,1)S(1)} collective-permute-done((bf16[512,2048]{1,0:T(8,128)(2,1)}, bf16[512,2048]{1,0:T(8,128)(2,1)S(1)}, u32[]{:S(2)}, u32[]{:S(2)}) %collective-permute-start.6) | collective-permute-done | bytes 2097184 | tf_op jit(solution)/shard_map/ppermute | solution.py:17
  480.6 12.4 %fusion.5 = f32[384,2048]{1,0:T(8,128)} fusion(bf16[4096,2048]{1,0:T(8,128)(2,1)} %all-gather.6.cloned.1.call-done, bf16[384,4096]{1,0:T(8,128)(2,1)} %all-gather.4.cloned.1.call-done, f32[4096]{0:T(1024)S(1)} %convert_element_type.40, f32[384]{0:T(512)S(1)} %add_rsqrt_fusion), kind=kOutput, calls=%fused_computation.13 | convolution fusion | flops 6448742400 | bytes 23086592 | tf_op jit(solution)/shard_map/dot_general | solution.py:40
  493.0 219.5 %all-gather.8.cloned.1.call-done = bf16[2048,4096]{1,0:T(8,128)(2,1)} async-done(((bf16[2048,512]{1,0:T(8,128)(2,1)}), bf16[2048,4096]{1,0:T(8,128)(2,1)}) %all-gather.8.cloned.1.call-update) | async-done | bytes 16777232 | tf_op jit(solution)/shard_map/all_gather | solution.py:48
  712.5 26.3 %convolution_convert_fusion = bf16[384,4096]{1,0:T(8,128)(2,1)} fusion(bf16[2048,4096]{1,0:T(8,128)(2,1)} %all-gather.8.cloned.1.call-done, f32[384,2048]{1,0:T(8,128)} %fusion.5, bf16[4096,2048]{1,0:T(8,128)(2,1)} %constant_dynamic-update-slice_fusion, bf16[384,4096]{1,0:T(8,128)(2,1)} %all-gather.4.cloned.1.call-done, f32[4096]{0:T(1024)S(1)} %convert_element_type.40, ...), kind=kOutput, calls=%fused_computation.7 | convolution fusion | flops 12897484800 | bytes 43009536 | tf_op jit(solution)/shard_map/dot_general | solution.py:46
  739.6 7.9 %gather_fusion.1 = bf16[512,1024]{1,0:T(8,128)(2,1)} fusion(bf16[8,64,1024]{2,1,0:T(8,128)(2,1)S(1)} %bitcast.16, s32[512]{0:T(512)S(1)} %reshape.116), kind=kCustom, calls=%fused_computation.1 | custom fusion | bytes 2101248 | tf_op jit(solution)/shard_map/vmap()/gather | solution.py:69
  747.6 27.3 %reduce-scatter.2.cloned.1.call-done = bf16[384,1024]{1,0:T(8,128)(2,1)} async-done(((bf16[384,4096]{1,0:T(8,128)(2,1)}), bf16[384,1024]{1,0:T(8,128)(2,1)}) %reduce-scatter.2.cloned.1.call-update) | async-done | bytes 786448 | tf_op jit(solution)/shard_map/reduce_scatter | solution.py:51
  776.2 2.7 gather_fusion
  778.9 3.6 fusion.4
  (47 shorter events, 17.4 us)
Async XLA Ops:
  6.5 733.0 %copy-start = (bf16[512,1024]{1,0:T(8,128)(2,1)S(1)}, bf16[512,1024]{1,0:T(8,128)(2,1)}, u32[]{:S(2)}) copy-start(bf16[512,1024]{1,0:T(8,128)(2,1)} %param.9) | copy-start | bytes 3145732
  6.5 404.1 %all-gather.4.cloned.1.call-start = ((), (), s32[]{:S(2)}) async-start(), calls=%async_computation.1 | async-start | bytes 3932160 | tf_op jit(solution)/shard_map/all_gather | solution.py:29
  8.1 4.4 copy-start.1
  10.9 251.0 %copy-start.5 = (bf16[1024]{0:T(1024)(128)(2,1)S(1)}, bf16[1024]{0:T(1024)(128)(2,1)}, u32[]{:S(2)}) copy-start(bf16[1024]{0:T(1024)(128)(2,1)} %param.10) | copy-start | bytes 6148
  11.0 469.6 %all-gather.6.cloned.1.call-start = ((), (), s32[]{:S(2)}) async-start(), calls=%async_computation.2 | async-start | bytes 18874368 | tf_op jit(solution)/shard_map/all_gather | solution.py:42
  11.7 700.8 %all-gather.8.cloned.1.call-start = ((), (), s32[]{:S(2)}) async-start(), calls=%async_computation.3 | async-start | bytes 18874368 | tf_op jit(solution)/shard_map/all_gather | solution.py:48
  12.5 762.4 %reduce-scatter.2.cloned.1.call-start = ((), (), s32[]{:S(2)}) async-start(), calls=%async_computation.4 | async-start | bytes 3932160 | tf_op jit(solution)/shard_map/reduce_scatter | solution.py:51
  12.5 115.3 %collective-permute-start = (bf16[512,2048]{1,0:T(8,128)(2,1)S(1)}, bf16[512,2048]{1,0:T(8,128)(2,1)S(1)}, u32[]{:S(2)}, u32[]{:S(2)}) collective-permute-start(bf16[512,2048]{1,0:T(8,128)(2,1)S(1)} %copy-done.1), channel_id=1, source_target_pairs={{0,4},{4,8},{8,12},{12,16},{16,20},{20,24},{24,28},{28,0},{1,5},{5... | collective-permute-start | bytes 6291464 | tf_op jit(solution)/shard_map/ppermute | solution.py:17
  15.5 114.8 %collective-permute-start.1 = (bf16[512,2048]{1,0:T(8,128)(2,1)S(1)}, bf16[512,2048]{1,0:T(8,128)(2,1)}, u32[]{:S(2)}, u32[]{:S(2)}) collective-permute-start(bf16[512,2048]{1,0:T(8,128)(2,1)S(1)} %copy-done.1), channel_id=1, source_target_pairs={{0,28},{4,0},{8,4},{12,8},{16,12},{20,16},{24,20},{28,24},{1,29},{... | collective-permute-start | bytes 6291464 | tf_op jit(solution)/shard_map/ppermute | solution.py:20
  127.8 2.5 copy-start.2
  127.8 131.5 %collective-permute-start.2 = (bf16[512,2048]{1,0:T(8,128)(2,1)S(1)}, bf16[512,2048]{1,0:T(8,128)(2,1)}, u32[]{:S(2)}, u32[]{:S(2)}) collective-permute-start(bf16[512,2048]{1,0:T(8,128)(2,1)S(1)} %collective-permute-done), channel_id=1, source_target_pairs={{0,4},{4,8},{8,12},{12,16},{16,20},{20,24},{24,28},{28,0},{1,5},{5... | collective-permute-start | bytes 6291464 | tf_op jit(solution)/shard_map/ppermute | solution.py:17
  130.3 136.8 %collective-permute-start.3 = (bf16[512,2048]{1,0:T(8,128)(2,1)}, bf16[512,2048]{1,0:T(8,128)(2,1)}, u32[]{:S(2)}, u32[]{:S(2)}) collective-permute-start(bf16[512,2048]{1,0:T(8,128)(2,1)} %collective-permute-done.1), channel_id=1, source_target_pairs={{0,28},{4,0},{8,4},{12,8},{16,12},{20,16},{24,20},{28,24},{1,29},{... | collective-permute-start | bytes 6291464 | tf_op jit(solution)/shard_map/ppermute | solution.py:20
  259.4 137.8 %collective-permute-start.4 = (bf16[512,2048]{1,0:T(8,128)(2,1)}, bf16[512,2048]{1,0:T(8,128)(2,1)}, u32[]{:S(2)}, u32[]{:S(2)}) collective-permute-start(bf16[512,2048]{1,0:T(8,128)(2,1)} %collective-permute-done.2), channel_id=1, source_target_pairs={{0,4},{4,8},{8,12},{12,16},{16,20},{20,24},{24,28},{28,0},{1,5},{5... | collective-permute-start | bytes 6291464 | tf_op jit(solution)/shard_map/ppermute | solution.py:17
  267.1 149.3 %collective-permute-start.5 = (bf16[512,2048]{1,0:T(8,128)(2,1)}, bf16[512,2048]{1,0:T(8,128)(2,1)}, u32[]{:S(2)}, u32[]{:S(2)}) collective-permute-start(bf16[512,2048]{1,0:T(8,128)(2,1)} %collective-permute-done.3), channel_id=1, source_target_pairs={{0,28},{4,0},{8,4},{12,8},{16,12},{20,16},{24,20},{28,24},{1,29},{... | collective-permute-start | bytes 6291464 | tf_op jit(solution)/shard_map/ppermute | solution.py:20
  289.8 109.9 %copy-start.3 = (bf16[512,2048]{1,0:T(8,128)(2,1)S(1)}, bf16[512,2048]{1,0:T(8,128)(2,1)}, u32[]{:S(2)}) copy-start(bf16[512,2048]{1,0:T(8,128)(2,1)} %copy-done.2) | copy-start | bytes 6291460
  397.2 81.8 %collective-permute-start.6 = (bf16[512,2048]{1,0:T(8,128)(2,1)}, bf16[512,2048]{1,0:T(8,128)(2,1)S(1)}, u32[]{:S(2)}, u32[]{:S(2)}) collective-permute-start(bf16[512,2048]{1,0:T(8,128)(2,1)} %collective-permute-done.4), channel_id=1, source_target_pairs={{0,4},{4,8},{8,12},{12,16},{16,20},{20,24},{24,28},{28,0},{1,5},{5... | collective-permute-start | bytes 6291464 | tf_op jit(solution)/shard_map/ppermute | solution.py:17
  738.8 0.7 copy-start.4
Sparse Core Ops, SparseCore 0:
  11.1 31.2 all-gather.3
  44.5 424.0 all-gather.5
  470.6 241.8 all-gather.7
  739.0 35.8 reduce-scatter.1
